TPU v7x, 32 devices: a whole 2x2x4 slice. The times are simulated.
32 devices in a mesh: feed: 4 (over y, core), tm: 8 (over z, x).
Axes of the slice: x: 2, y: 2, z: 4, core: 2. Of those that a mesh axis runs over, the one named last changes fastest.
Arguments:
- tod: bfloat16 [8192, 50, 256], P(('feed', 'tm')), may hold values from -6 to 6
- pixels: int32 [8192, 50], P(('feed', 'tm')), may hold values from 0 to 31
- block_slots: int32 [8192], P(('feed', 'tm')), may hold values from 0 to 7, as said below
- tile_lists: int32 [32, 8, 1], P(('feed', 'tm')), may hold values from -1 to 63, as said below
- tile_place: int32 [64], replicated, may hold values from 0 to 63, as said below
- prior: float32 [256], replicated, may hold values from 0.5 to 4
Outputs:
- drift_levels: float32 [8192, 256], P(('feed', 'tm'))
- leftover_error: float32 [8192, 256], P(('feed', 'tm'))
- destriped_result_map: float32 [64, 32, 256], P('tm', None, 'feed')
Inputs may be any that keep to these rules, and one draw needn't show every extreme that they name: tile_lists[g, o, s] is -1 or a tile whose tile_place // 8 equals o; the live entries of one device are distinct; entries 0 and 7 of each device's flattened list are live; some tiles are named by no list. block_slots[b] names a live entry of the flattened list of the device that holds baseline b. tile_place is a permutation of the tiles; place p is stored by tm index p // 8 in its row p % 8.
All inputs are finite; a program needn't handle non-finite values.
Results may differ from a plain program's by a relative error of at most 0.0013.
Values sent between devices are 32-bit elements; how exact they have to be, the bound alone decides.
No kernel may reach another device: no remote copies, remote signals or barrier semaphores. Data moves between devices by JAX's collectives and lax.ppermute only.
A program may use at most 64 MiB of HBM per device.

v0:
```python
import jax
import jax.numpy as jnp
from jax import lax
from jax.sharding import PartitionSpec as P

CELLS_IN_PATCH = 32
ITERS = 2


def local(tod, pixels, block_slots, tile_lists, tile_place, prior):
    highest = lax.Precision.HIGHEST
    tm_count = lax.axis_size("tm")
    feed_count = lax.axis_size("feed")
    slot_count = tile_lists.shape[1] * tile_lists.shape[2]
    tile_total = tile_place.shape[0]
    rows_owned = tile_total // tm_count
    owner_index = lax.axis_index("tm")
    block_count = tod.shape[0]
    sample_count = tod.shape[1]
    channels = tod.shape[2]
    share_width = channels // feed_count
    pix_match = pixels[:, :, None] == jnp.arange(CELLS_IN_PATCH, dtype=jnp.int32)[None, None, :]
    hit_blocks = jnp.sum(pix_match.astype(jnp.float32), axis=1)
    slot_hot = (block_slots[:, None] == jnp.arange(slot_count, dtype=jnp.int32)[None, :]).astype(
        jnp.float32
    )
    weights = (slot_hot[:, :, None] * hit_blocks[:, None, :]).reshape(
        block_count, slot_count * CELLS_IN_PATCH
    )
    hit_slots = jnp.sum(weights, axis=0).reshape(slot_count, CELLS_IN_PATCH)
    my_list = tile_lists.reshape(slot_count)
    recv_hits, recv_tiles = (
        lax.all_to_all(hit_slots, "tm", split_axis=0, concat_axis=0, tiled=True),
        lax.all_to_all(my_list, "tm", split_axis=0, concat_axis=0, tiled=True),
    )
    matches = recv_tiles[:, None] == jnp.arange(tile_total, dtype=jnp.int32)[None, :]
    recv_place = jnp.sum(jnp.where(matches, tile_place[None, :] + 1, 0), axis=1) - 1
    local_rows = owner_index * rows_owned + jnp.arange(rows_owned, dtype=jnp.int32)
    select = (local_rows[:, None] == recv_place[None, :]).astype(jnp.float32)
    owned_hits = jnp.dot(select, recv_hits, precision=highest)
    hits = lax.psum(owned_hits, "feed")
    inverse = 1.0 / jnp.maximum(hits, 1.0)

    def averaged_patch_lines(slot_parts):
        received = lax.all_to_all(slot_parts, "tm", split_axis=0, concat_axis=0, tiled=True)
        owned_sum = jnp.einsum("lk,kpc->lpc", select, received, precision=highest)
        summed = lax.psum(owned_sum, "feed")
        return summed * inverse[:, :, None]

    def project(slot_parts, sample_sums):
        sky_tiles = averaged_patch_lines(slot_parts)
        outgoing = jnp.einsum("lk,lpc->kpc", select, sky_tiles, precision=highest)
        returned = lax.all_to_all(outgoing, "tm", split_axis=0, concat_axis=0, tiled=True)
        flat_tiles = returned.reshape(slot_count * CELLS_IN_PATCH, channels)
        mapped = jnp.dot(weights, flat_tiles, precision=highest)
        return sample_sums - mapped

    def unrolled_drift_levels(values):
        parts_flat = jnp.einsum("bq,bc->qc", weights, values, precision=highest)
        return parts_flat.reshape(slot_count, CELLS_IN_PATCH, channels)

    def squares(values):
        return lax.psum(jnp.sum(values * values), ("feed", "tm"))

    pix_hot = pix_match.astype(jnp.bfloat16)
    per_block = jnp.einsum("bsp,bsc->bpc", pix_hot, tod, preferred_element_type=jnp.float32)
    observation_segments = jnp.einsum("bk,bpc->kpc", slot_hot, per_block, precision=highest)
    data_sums = jnp.sum(per_block, axis=1)
    system_target = project(observation_segments, data_sums)
    drift_levels = jnp.zeros_like(system_target)
    leftover_error = system_target
    descent_direction = system_target
    norm_now = squares(leftover_error)
    for number in range(ITERS):
        image = (
            project(unrolled_drift_levels(descent_direction), sample_count * descent_direction)
            + prior[None, :] * descent_direction
        )
        update_factor = norm_now / lax.psum(jnp.sum(descent_direction * image), ("feed", "tm"))
        drift_levels = drift_levels + update_factor * descent_direction
        leftover_error = leftover_error - update_factor * image
        norm_next = squares(leftover_error)
        descent_direction = leftover_error + norm_next / norm_now * descent_direction
        norm_now = norm_next
    converged_patch_lines = averaged_patch_lines(
        observation_segments - unrolled_drift_levels(drift_levels)
    )
    destriped_result_map = lax.dynamic_slice_in_dim(
        converged_patch_lines, lax.axis_index("feed") * share_width, share_width, 2
    )
    return (drift_levels, leftover_error, destriped_result_map)


def solution(mesh):
    return jax.shard_map(
        local,
        mesh=mesh,
        in_specs=(
            P(("feed", "tm"), None, None),
            P(("feed", "tm"), None),
            P(("feed", "tm")),
            P(("feed", "tm"), None, None),
            P(),
            P(),
        ),
        out_specs=(P(("feed", "tm"), None), P(("feed", "tm"), None), P("tm", None, "feed")),
        check_vma=False,
    )
```

profile of v0, /device:TPU:0, one launch (start us, length us, event | category | flops | bytes accessed | tf_op | source)
XLA Modules:
  0.0 404.3 jit_solution(7255400728901228236)
XLA Ops:
  7.2 1.3 copy.88
  8.5 7.3 %all-to-all-start = ((s32[8,1,1]{2,1,0:T(1,128)}), s32[8,1,1]{2,1,0:T(1,128)S(1)}, u32[]{:S(2)}, u32[]{:S(2)}) async-start(s32[8,1,1]{2,1,0:T(1,128)} %copy.88), calls=%async_computation | async-start | bytes 8192 | tf_op jit(solution)/shard_map/all_to_all | solution.py:34
  15.8 0.9 copy.85
  16.7 1.2 convert_reduce_fusion
  17.9 7.7 %fusion.54 = (f32[256,256]{1,0:T(8,128)S(1)}, f32[256,32,256]{2,1,0:T(8,128)S(1)}) fusion(bf16[256,50,256]{2,0,1:T(8,128)(2,1)} %param.6, s32[256,50]{1,0:T(8,128)S(1)} %copy.85), kind=kOutput, calls=%fused_computation.78 | convolution fusion | flops 212156416 | bytes 15255552 | tf_op jit(solution)/shard_map/bsp,bsc->bpc/dot_general | solution.py:66
  25.6 7.7 %fusion = f32[8,32,256]{2,0,1:T(8,128)S(1)} fusion(f32[256,32,256]{2,1,0:T(8,128)S(1)} %get-tuple-element.30, s32[256]{0:T(256)S(1)} %copy-done.1), kind=kOutput, calls=%fused_computation | convolution fusion | flops 201328640 | bytes 8651776 | tf_op jit(solution)/shard_map/bk,bpc->kpc/dot_general | solution.py:67
  33.4 0.7 multiply_bitcast_fusion
  34.1 6.0 %all-to-all-start.2 = ((f32[8,1,32]{2,1,0:T(1,128)}), f32[8,1,32]{2,1,0:T(1,128)S(1)}, u32[]{:S(2)}, u32[]{:S(2)}) async-start(f32[8,1,32]{2,1,0:T(1,128)} %bitcast.4), calls=%async_computation.2 | async-start | bytes 8192 | tf_op jit(solution)/shard_map/all_to_all | solution.py:33
  40.1 0.8 copy.90
  40.9 0.2 reduce.1
  41.1 5.4 %all-to-all-done.2 = f32[8,1,32]{2,1,0:T(1,128)S(1)} async-done(((f32[8,1,32]{2,1,0:T(1,128)}), f32[8,1,32]{2,1,0:T(1,128)S(1)}, u32[]{:S(2)}, u32[]{:S(2)}) %all-to-all-start.2) | async-done | bytes 1056 | tf_op jit(solution)/shard_map/all_to_all | solution.py:33
  46.5 3.4 all-to-all-start.1
  50.0 0.2 select_reduce_fusion
  50.2 0.2 fusion.49
  50.4 5.9 %psum.64 = f32[8,32]{1,0:T(8,128)S(1)} all-reduce(f32[8,32]{1,0:T(8,128)S(1)} %fusion.49), channel_id=1, replica_groups=mesh['feed'=4,'tm'=8] {'feed'}, use_global_device_ids=true, to_apply=%region_5.6 | all-reduce | flops 256 | bytes 2048 | tf_op jit(solution)/shard_map/psum | solution.py:41
  56.3 1.8 all-to-all-done.1
  58.1 1.1 fusion.25
  59.4 31.9 %all-reduce.6.cloned.1.call-done = f32[8,32,256]{2,0,1:T(8,128)} async-done(((f32[8,32,256]{2,0,1:T(8,128)}), f32[8,32,256]{2,0,1:T(8,128)}) %all-reduce.6.cloned.1.call-update) | async-done | bytes 262160 | tf_op jit(solution)/shard_map/psum | solution.py:47
  91.2 1.3 fusion.31
  92.7 13.5 %all_to_all.56 = f32[8,32,256]{2,1,0:T(8,128)S(1)} all-to-all(f32[8,32,256]{2,1,0:T(8,128)S(1)} %copy.94), channel_id=1, replica_groups=mesh['feed'=4,'tm'=8] {'tm'}, dimensions={0} | all-to-all | bytes 524288 | tf_op jit(solution)/shard_map/all_to_all | solution.py:53
  106.2 0.6 fusion.5
  106.8 0.4 fusion.16
  107.2 11.1 %all_to_all.57 = f32[8,32,256]{2,1,0:T(8,128)S(1)} all-to-all(f32[8,32,256]{2,1,0:T(8,128)S(1)} %fusion.16), channel_id=1, replica_groups=mesh['feed'=4,'tm'=8] {'tm'}, dimensions={0} | all-to-all | bytes 524288 | tf_op jit(solution)/shard_map/all_to_all | solution.py:45
  118.3 1.1 fusion.23
  119.5 31.2 %all-reduce.8.cloned.1.call-done = f32[8,32,256]{2,0,1:T(8,128)} async-done(((f32[8,32,256]{2,0,1:T(8,128)}), f32[8,32,256]{2,0,1:T(8,128)}) %all-reduce.8.cloned.1.call-update) | async-done | bytes 262160 | tf_op jit(solution)/shard_map/psum | solution.py:47
  150.8 1.3 fusion.29
  152.2 13.5 %all_to_all.58 = f32[8,32,256]{2,1,0:T(8,128)S(1)} all-to-all(f32[8,32,256]{2,1,0:T(8,128)S(1)} %copy.97), channel_id=1, replica_groups=mesh['feed'=4,'tm'=8] {'tm'}, dimensions={0} | all-to-all | bytes 524288 | tf_op jit(solution)/shard_map/all_to_all | solution.py:53
  165.7 1.2 multiply_reduce_fusion.3
  167.0 38.0 %all-reduce = (f32[]{:T(128)}, f32[]{:T(128)}) all-reduce(f32[]{:T(128)} %get-tuple-element.22, f32[]{:T(128)} %get-tuple-element.21), channel_id=1, replica_groups=mesh['feed'=4,'tm'=8] {'feed','tm'}, use_global_device_ids=true, to_apply=%region_7.8 | all-reduce | flops 2 | bytes 16 | tf_op jit(solution)/shard_map/psum | solution.py:63
  206.3 0.7 multiply_reduce_fusion.2
  207.0 41.4 %psum.68 = f32[]{:T(128)} all-reduce(f32[]{:T(128)} %multiply_reduce_fusion.2), channel_id=1, replica_groups=mesh['feed'=4,'tm'=8] {'feed','tm'}, use_global_device_ids=true, to_apply=%region_12.13 | all-reduce | flops 1 | bytes 8 | tf_op jit(solution)/shard_map/psum | solution.py:63
  249.8 0.4 fusion.14
  250.2 12.5 %all_to_all.59 = f32[8,32,256]{2,1,0:T(8,128)S(1)} all-to-all(f32[8,32,256]{2,1,0:T(8,128)S(1)} %fusion.14), channel_id=1, replica_groups=mesh['feed'=4,'tm'=8] {'tm'}, dimensions={0} | all-to-all | bytes 524288 | tf_op jit(solution)/shard_map/all_to_all | solution.py:45
  262.7 1.1 fusion.21
  263.9 30.5 %all-reduce.10.cloned.1.call-done = f32[8,32,256]{2,0,1:T(8,128)} async-done(((f32[8,32,256]{2,0,1:T(8,128)}), f32[8,32,256]{2,0,1:T(8,128)}) %all-reduce.10.cloned.1.call-update) | async-done | bytes 262160 | tf_op jit(solution)/shard_map/psum | solution.py:47
  294.4 1.3 fusion.27
  295.8 0.1 copy.100
  295.9 13.5 %all_to_all.60 = f32[8,32,256]{2,1,0:T(8,128)S(1)} all-to-all(f32[8,32,256]{2,1,0:T(8,128)S(1)} %copy.100), channel_id=1, replica_groups=mesh['feed'=4,'tm'=8] {'tm'}, dimensions={0} | all-to-all | bytes 524288 | tf_op jit(solution)/shard_map/all_to_all | solution.py:53
  309.4 1.2 multiply_reduce_fusion.1
  310.6 37.9 %psum.70 = f32[]{:T(128)} all-reduce(f32[]{:T(128)} %get-tuple-element.32), channel_id=1, replica_groups=mesh['feed'=4,'tm'=8] {'feed','tm'}, use_global_device_ids=true, to_apply=%region_15.16 | all-reduce | flops 1 | bytes 8 | tf_op jit(solution)/shard_map/psum | solution.py:79
  349.9 0.8 multiply_subtract_fusion
  350.7 0.5 convolution_subtract_fusion
  351.2 0.1 copy.102
  351.3 13.1 %all_to_all.61 = f32[8,32,256]{2,1,0:T(8,128)S(1)} all-to-all(f32[8,32,256]{2,1,0:T(8,128)S(1)} %copy.102), channel_id=1, replica_groups=mesh['feed'=4,'tm'=8] {'tm'}, dimensions={0} | all-to-all | bytes 524288 | tf_op jit(solution)/shard_map/all_to_all | solution.py:45
  364.3 1.1 fusion.18
  365.5 30.6 %all-reduce.12.cloned.1.call-done = f32[8,32,256]{2,0,1:T(8,128)} async-done(((f32[8,32,256]{2,0,1:T(8,128)}), f32[8,32,256]{2,0,1:T(8,128)}) %all-reduce.12.cloned.1.call-update) | async-done | bytes 262160 | tf_op jit(solution)/shard_map/psum | solution.py:47
  396.1 1.0 dynamic-slice_multiply_fusion
  397.1 0.7 copy.104
  (26 shorter events, 0.6 us)
Async XLA Ops:
  8.5 25.6 %all-to-all-start = ((s32[8,1,1]{2,1,0:T(1,128)}), s32[8,1,1]{2,1,0:T(1,128)S(1)}, u32[]{:S(2)}, u32[]{:S(2)}) async-start(s32[8,1,1]{2,1,0:T(1,128)} %copy.88), calls=%async_computation | async-start | bytes 8192 | tf_op jit(solution)/shard_map/all_to_all | solution.py:34
  17.8 7.8 %copy-start.1 = (s32[256]{0:T(256)S(1)}, s32[256]{0:T(256)}, u32[]{:S(2)}) copy-start(s32[256]{0:T(256)} %param.8) | copy-start | bytes 3076
  25.6 14.5 %copy-start.3 = (s32[64]{0:T(128)S(1)}, s32[64]{0:T(128)}, u32[]{:S(2)}) copy-start(s32[64]{0:T(128)} %param.10) | copy-start | bytes 772
  25.6 140.1 %copy-start.2 = (f32[256]{0:T(256)S(1)}, f32[256]{0:T(256)}, u32[]{:S(2)}) copy-start(f32[256]{0:T(256)} %param.11) | copy-start | bytes 3076
  34.1 12.4 %all-to-all-start.2 = ((f32[8,1,32]{2,1,0:T(1,128)}), f32[8,1,32]{2,1,0:T(1,128)S(1)}, u32[]{:S(2)}, u32[]{:S(2)}) async-start(f32[8,1,32]{2,1,0:T(1,128)} %bitcast.4), calls=%async_computation.2 | async-start | bytes 8192 | tf_op jit(solution)/shard_map/all_to_all | solution.py:33
  46.5 11.6 %all-to-all-start.1 = ((f32[8,32,256]{2,1,0:T(8,128)}), f32[8,32,256]{2,1,0:T(8,128)S(1)}, u32[]{:S(2)}, u32[]{:S(2)}) async-start(f32[8,32,256]{2,1,0:T(8,128)} %copy.90), calls=%async_computation.1 | async-start | bytes 524288 | tf_op jit(solution)/shard_map/all_to_all | solution.py:45
  49.9 41.3 %all-reduce.6.cloned.1.call-start = ((), (), s32[]{:S(2)}) async-start(), calls=%async_computation.9 | async-start | bytes 524288 | tf_op jit(solution)/shard_map/psum | solution.py:47
  59.2 91.5 %all-reduce.8.cloned.1.call-start = ((), (), s32[]{:S(2)}) async-start(), calls=%async_computation.10 | async-start | bytes 524288 | tf_op jit(solution)/shard_map/psum | solution.py:47
  119.5 174.9 %all-reduce.10.cloned.1.call-start = ((), (), s32[]{:S(2)}) async-start(), calls=%async_computation.11 | async-start | bytes 524288 | tf_op jit(solution)/shard_map/psum | solution.py:47
  263.8 132.2 %all-reduce.12.cloned.1.call-start = ((), (), s32[]{:S(2)}) async-start(), calls=%async_computation.12 | async-start | bytes 524288 | tf_op jit(solution)/shard_map/psum | solution.py:47
  350.7 47.1 %copy-start = (f32[256,256]{1,0:T(8,128)}, f32[256,256]{1,0:T(8,128)S(1)}, u32[]{:S(2)}) copy-start(f32[256,256]{1,0:T(8,128)S(1)} %get-tuple-element.26) | copy-start | bytes 786436
Sparse Core Ops, SparseCore 0:
  59.4 31.8 all-reduce.5
  119.6 31.1 all-reduce.7
  264.0 30.4 all-reduce.9
  365.6 30.4 all-reduce.11
where the time goes:
time: 405 us; the launch traced here: 404 us
  blocking collectives  201 us (50%)
  waiting for transfers between devices  131 us (32%)
  matrix products  28.3 us (7%)
  between operations  18 us (4%)
  starting transfers between devices  16.9 us (4%)
  other arithmetic  4.82 us (1%)
  local copies, waits for them, and re-layouts  4.22 us (1%)
    psum x4, waiting for transfers between devices, averaged_patch_lines(): summed = lax.psum(owned_sum, 'feed')  124 us
    psum x2, blocking collectives, squares(): return lax.psum(jnp.sum(values * values), ('feed', 'tm'))  79.4 us
    all_to_all x3, blocking collectives, project(): lax.all_to_all(outgoing, 'tm', split_axis=0, concat_axis=0, tiled=True)  40.6 us
    psum x1, blocking collectives, local(): lax.psum(jnp.sum(descent_direction * image), ('feed', 'tm'))  37.9 us
    all_to_all x3, blocking collectives, averaged_patch_lines(): lax.all_to_all(slot_parts, 'tm', split_axis=0, concat_axis=0, tiled=True)  36.8 us
  transfers between devices with their start and end apart: 7, of which 6 were waited for; matrix products, arithmetic and copies ran while one was open for 5% of the time, Pallas kernels for 0%

commit v1 on v0

--- a/solution.py
+++ b/solution.py
@@ -44,7 +44,8 @@
     def averaged_patch_lines(slot_parts):
         received = lax.all_to_all(slot_parts, "tm", split_axis=0, concat_axis=0, tiled=True)
         owned_sum = jnp.einsum("lk,kpc->lpc", select, received, precision=highest)
-        summed = lax.psum(owned_sum, "feed")
+        pieces = lax.all_gather(owned_sum, "feed", axis=0, tiled=False)
+        summed = pieces.sum(axis=0)
         return summed * inverse[:, :, None]
 
     def project(slot_parts, sample_sums):

time: 405 us -> 338 us (0.83)
  waiting for transfers between devices: 131 us -> 52.9 us
  blocking collectives: 201 us -> 214 us
    psum x4 -> x0, waiting for transfers between devices: 124 us -> none  [averaged_patch_lines(): summed = lax.psum(owned_sum, 'feed')]
    all_gather x0 -> x4, waiting for transfers between devices: none -> 44.8 us  [averaged_patch_lines(): pieces = lax.all_gather(owned_sum, 'feed', axis=0, tiled=False)]
    all_to_all x0 -> x1, blocking collectives: none -> 9.73 us  [local(): lax.all_to_all(hit_slots, 'tm', split_axis=0, concat_axis=0, tiled=True)]
    all_to_all x1, waiting for transfers between devices: 1.8 us -> 8.01 us  [averaged_patch_lines(): lax.all_to_all(slot_parts, 'tm', split_axis=0, concat_axis=0, tiled=True)]
    all_to_all x1 -> x0, starting transfers between devices: 6 us -> none  [local(): lax.all_to_all(hit_slots, 'tm', split_axis=0, concat_axis=0, tiled=True)]
    all_to_all x1 -> x0, waiting for transfers between devices: 5.38 us -> none  [local(): lax.all_to_all(hit_slots, 'tm', split_axis=0, concat_axis=0, tiled=True)]
    reduce_sum x0 -> x4, other arithmetic: none -> 5.29 us  [averaged_patch_lines(): summed = pieces.sum(axis=0)]
  transfers between devices with their start and end apart: 7 -> 6, of which waited for: 6 -> 4; matrix products, arithmetic and copies ran while one was open for 5% -> 6% of each run, Pallas kernels for 0% -> 0%
where the time goes in v1:
time: 338 us; the launch traced here: 337 us
  blocking collectives  214 us (63%)
  waiting for transfers between devices  52.9 us (16%)
  matrix products  25.5 us (8%)
  between operations  18 us (5%)
  starting transfers between devices  13.4 us (4%)
  other arithmetic  8.63 us (3%)
  local copies, waits for them, and re-layouts  4.22 us (1%)
    psum x2, blocking collectives, squares(): return lax.psum(jnp.sum(values * values), ('feed', 'tm'))  79.7 us
    all_gather x4, waiting for transfers between devices, averaged_patch_lines(): pieces = lax.all_gather(owned_sum, 'feed', axis=0, tiled=False)  44.8 us
    all_to_all x3, blocking collectives, project(): lax.all_to_all(outgoing, 'tm', split_axis=0, concat_axis=0, tiled=True)  42.7 us
    psum x1, blocking collectives, local(): lax.psum(jnp.sum(descent_direction * image), ('feed', 'tm'))  38.9 us
    all_to_all x3, blocking collectives, averaged_patch_lines(): lax.all_to_all(slot_parts, 'tm', split_axis=0, concat_axis=0, tiled=True)  37.4 us
    all_to_all x1, blocking collectives, local(): lax.all_to_all(hit_slots, 'tm', split_axis=0, concat_axis=0, tiled=True)  9.73 us
    all_to_all x1, waiting for transfers between devices, averaged_patch_lines(): lax.all_to_all(slot_parts, 'tm', split_axis=0, concat_axis=0, tiled=True)  8.01 us
    dot_general x1, matrix products, local(): jnp.einsum('bsp,bsc->bpc', pix_hot, tod, preferred_element_type=jnp.float32)  7.73 us
  transfers between devices with their start and end apart: 6, of which 4 were waited for; matrix products, arithmetic and copies ran while one was open for 6% of the time, Pallas kernels for 0%

profile of v1, /device:TPU:0, one launch (start us, length us, event | category | flops | bytes accessed | tf_op | source)
XLA Modules:
  0.0 336.7 jit_solution(12535671078461442411)
XLA Ops:
  7.2 1.3 copy.89
  8.5 7.3 %all-to-all-start = ((s32[8,1,1]{2,1,0:T(1,128)}), s32[8,1,1]{2,1,0:T(1,128)S(1)}, u32[]{:S(2)}, u32[]{:S(2)}) async-start(s32[8,1,1]{2,1,0:T(1,128)} %copy.89), calls=%async_computation | async-start | bytes 8192 | tf_op jit(solution)/shard_map/all_to_all | solution.py:34
  15.8 0.9 copy.86
  16.7 7.7 %fusion.54 = (f32[256,256]{1,0:T(8,128)S(1)}, f32[256,32,256]{2,1,0:T(8,128)S(1)}) fusion(bf16[256,50,256]{2,0,1:T(8,128)(2,1)} %param.6, s32[256,50]{1,0:T(8,128)S(1)} %copy.86), kind=kOutput, calls=%fused_computation.82 | convolution fusion | flops 212156416 | bytes 15255552 | tf_op jit(solution)/shard_map/bsp,bsc->bpc/dot_general | solution.py:67
  24.5 7.7 %fusion = f32[8,32,256]{2,0,1:T(8,128)S(1)} fusion(f32[256,32,256]{2,1,0:T(8,128)S(1)} %get-tuple-element.27, s32[256]{0:T(256)S(1)} %copy-done.1), kind=kOutput, calls=%fused_computation | convolution fusion | flops 201328640 | bytes 8651776 | tf_op jit(solution)/shard_map/bk,bpc->kpc/dot_general | solution.py:68
  32.1 0.8 copy.91
  32.9 6.0 %all-to-all-start.1 = ((f32[8,32,256]{2,1,0:T(8,128)}), f32[8,32,256]{2,1,0:T(8,128)S(1)}, u32[]{:S(2)}, u32[]{:S(2)}) async-start(f32[8,32,256]{2,1,0:T(8,128)} %copy.91), calls=%async_computation.1 | async-start | bytes 524288 | tf_op jit(solution)/shard_map/all_to_all | solution.py:45
  39.0 0.2 reduce.1
  39.2 0.2 select_reduce_fusion
  39.4 8.0 %all-to-all-done.1 = f32[8,32,256]{2,1,0:T(8,128)S(1)} async-done(((f32[8,32,256]{2,1,0:T(8,128)}), f32[8,32,256]{2,1,0:T(8,128)S(1)}, u32[]{:S(2)}, u32[]{:S(2)}) %all-to-all-start.1) | async-done | bytes 262176 | tf_op jit(solution)/shard_map/all_to_all | solution.py:45
  47.4 1.1 fusion.25
  48.6 1.2 convert_reduce_fusion
  49.9 0.1 multiply_bitcast_fusion
  50.0 9.7 %all_to_all.56 = f32[8,1,32]{2,1,0:T(1,128)S(1)} all-to-all(f32[8,1,32]{2,1,0:T(1,128)S(1)} %bitcast.63), channel_id=1, replica_groups=mesh['feed'=4,'tm'=8] {'tm'}, dimensions={0} | all-to-all | bytes 2048 | tf_op jit(solution)/shard_map/all_to_all | solution.py:33
  59.7 0.2 fusion.49
  59.9 5.6 %psum.35 = f32[8,32]{1,0:T(8,128)S(1)} all-reduce(f32[8,32]{1,0:T(8,128)S(1)} %fusion.49), channel_id=1, replica_groups=mesh['feed'=4,'tm'=8] {'feed'}, use_global_device_ids=true, to_apply=%region_5.6 | all-reduce | flops 256 | bytes 2048 | tf_op jit(solution)/shard_map/psum | solution.py:41
  65.6 1.3 bitcast_reduce_fusion.3
  66.9 0.4 fusion.31
  67.4 13.4 %all_to_all.57 = f32[8,32,256]{2,1,0:T(8,128)S(1)} all-to-all(f32[8,32,256]{2,1,0:T(8,128)S(1)} %copy.95), channel_id=1, replica_groups=mesh['feed'=4,'tm'=8] {'tm'}, dimensions={0} | all-to-all | bytes 524288 | tf_op jit(solution)/shard_map/all_to_all | solution.py:54
  80.9 0.6 fusion.5
  81.5 0.4 fusion.16
  81.9 12.3 %all_to_all.58 = f32[8,32,256]{2,1,0:T(8,128)S(1)} all-to-all(f32[8,32,256]{2,1,0:T(8,128)S(1)} %fusion.16), channel_id=1, replica_groups=mesh['feed'=4,'tm'=8] {'tm'}, dimensions={0} | all-to-all | bytes 524288 | tf_op jit(solution)/shard_map/all_to_all | solution.py:45
  94.1 1.1 fusion.23
  95.3 14.9 %all-gather.11.cloned.1.call-done = f32[32,32,256]{2,0,1:T(8,128)} async-done(((f32[8,32,256]{2,0,1:T(8,128)}), f32[32,32,256]{2,0,1:T(8,128)}) %all-gather.11.cloned.1.call-update) | async-done | bytes 1048592 | tf_op jit(solution)/shard_map/all_gather | solution.py:47
  110.2 1.3 bitcast_reduce_fusion.2
  111.5 0.4 fusion.29
  112.0 14.6 %all_to_all.59 = f32[8,32,256]{2,1,0:T(8,128)S(1)} all-to-all(f32[8,32,256]{2,1,0:T(8,128)S(1)} %copy.98), channel_id=1, replica_groups=mesh['feed'=4,'tm'=8] {'tm'}, dimensions={0} | all-to-all | bytes 524288 | tf_op jit(solution)/shard_map/all_to_all | solution.py:54
  126.6 1.2 multiply_reduce_fusion.3
  127.8 39.0 %all-reduce = (f32[]{:T(128)}, f32[]{:T(128)}) all-reduce(f32[]{:T(128)} %get-tuple-element.19, f32[]{:T(128)} %get-tuple-element.18), channel_id=1, replica_groups=mesh['feed'=4,'tm'=8] {'feed','tm'}, use_global_device_ids=true, to_apply=%region_7.8 | all-reduce | flops 2 | bytes 16 | tf_op jit(solution)/shard_map/psum | solution.py:64
  168.1 0.7 multiply_reduce_fusion.2
  168.8 40.7 %psum.38 = f32[]{:T(128)} all-reduce(f32[]{:T(128)} %multiply_reduce_fusion.2), channel_id=1, replica_groups=mesh['feed'=4,'tm'=8] {'feed','tm'}, use_global_device_ids=true, to_apply=%region_12.13 | all-reduce | flops 1 | bytes 8 | tf_op jit(solution)/shard_map/psum | solution.py:64
  210.9 0.4 fusion.14
  211.3 12.6 %all_to_all.60 = f32[8,32,256]{2,1,0:T(8,128)S(1)} all-to-all(f32[8,32,256]{2,1,0:T(8,128)S(1)} %fusion.14), channel_id=1, replica_groups=mesh['feed'=4,'tm'=8] {'tm'}, dimensions={0} | all-to-all | bytes 524288 | tf_op jit(solution)/shard_map/all_to_all | solution.py:45
  223.8 1.1 fusion.21
  225.0 15.0 %all-gather.13.cloned.1.call-done = f32[32,32,256]{2,0,1:T(8,128)} async-done(((f32[8,32,256]{2,0,1:T(8,128)}), f32[32,32,256]{2,0,1:T(8,128)}) %all-gather.13.cloned.1.call-update) | async-done | bytes 1048592 | tf_op jit(solution)/shard_map/all_gather | solution.py:47
  240.0 1.3 bitcast_reduce_fusion.1
  241.3 0.4 fusion.27
  241.8 14.6 %all_to_all.61 = f32[8,32,256]{2,1,0:T(8,128)S(1)} all-to-all(f32[8,32,256]{2,1,0:T(8,128)S(1)} %copy.101), channel_id=1, replica_groups=mesh['feed'=4,'tm'=8] {'tm'}, dimensions={0} | all-to-all | bytes 524288 | tf_op jit(solution)/shard_map/all_to_all | solution.py:54
  256.4 1.2 multiply_reduce_fusion.1
  257.6 38.9 %psum.39 = f32[]{:T(128)} all-reduce(f32[]{:T(128)} %get-tuple-element.29), channel_id=1, replica_groups=mesh['feed'=4,'tm'=8] {'feed','tm'}, use_global_device_ids=true, to_apply=%region_15.16 | all-reduce | flops 1 | bytes 8 | tf_op jit(solution)/shard_map/psum | solution.py:80
  297.9 0.8 multiply_subtract_fusion
  298.7 0.5 convolution_subtract_fusion
  299.3 12.6 %all_to_all.62 = f32[8,32,256]{2,1,0:T(8,128)S(1)} all-to-all(f32[8,32,256]{2,1,0:T(8,128)S(1)} %copy.103), channel_id=1, replica_groups=mesh['feed'=4,'tm'=8] {'tm'}, dimensions={0} | all-to-all | bytes 524288 | tf_op jit(solution)/shard_map/all_to_all | solution.py:45
  311.8 1.1 fusion.18
  313.0 15.0 %all-gather.15.cloned.1.call-done = f32[32,32,256]{2,0,1:T(8,128)} async-done(((f32[8,32,256]{2,0,1:T(8,128)}), f32[32,32,256]{2,0,1:T(8,128)}) %all-gather.15.cloned.1.call-update) | async-done | bytes 1048592 | tf_op jit(solution)/shard_map/all_gather | solution.py:47
  328.0 1.3 bitcast_reduce_fusion
  329.3 0.1 dynamic-slice_multiply_fusion
  329.5 0.7 copy.105
  (29 shorter events, 0.8 us)
Async XLA Ops:
  8.5 24.4 %all-to-all-start = ((s32[8,1,1]{2,1,0:T(1,128)}), s32[8,1,1]{2,1,0:T(1,128)S(1)}, u32[]{:S(2)}, u32[]{:S(2)}) async-start(s32[8,1,1]{2,1,0:T(1,128)} %copy.89), calls=%async_computation | async-start | bytes 8192 | tf_op jit(solution)/shard_map/all_to_all | solution.py:34
  16.7 7.8 %copy-start.1 = (s32[256]{0:T(256)S(1)}, s32[256]{0:T(256)}, u32[]{:S(2)}) copy-start(s32[256]{0:T(256)} %param.8) | copy-start | bytes 3076
  24.4 14.5 %copy-start.3 = (s32[64]{0:T(128)S(1)}, s32[64]{0:T(128)}, u32[]{:S(2)}) copy-start(s32[64]{0:T(128)} %param.10) | copy-start | bytes 772
  32.1 94.5 %copy-start.2 = (f32[256]{0:T(256)S(1)}, f32[256]{0:T(256)}, u32[]{:S(2)}) copy-start(f32[256]{0:T(256)} %param.11) | copy-start | bytes 3076
  32.9 14.5 %all-to-all-start.1 = ((f32[8,32,256]{2,1,0:T(8,128)}), f32[8,32,256]{2,1,0:T(8,128)S(1)}, u32[]{:S(2)}, u32[]{:S(2)}) async-start(f32[8,32,256]{2,1,0:T(8,128)} %copy.91), calls=%async_computation.1 | async-start | bytes 524288 | tf_op jit(solution)/shard_map/all_to_all | solution.py:45
  38.9 26.7 %all-gather.9.cloned.1.call-start = ((), (), s32[]{:S(2)}) async-start(), calls=%async_computation.9 | async-start | bytes 1310720 | tf_op jit(solution)/shard_map/all_gather | solution.py:47
  48.6 61.6 %all-gather.11.cloned.1.call-start = ((), (), s32[]{:S(2)}) async-start(), calls=%async_computation.10 | async-start | bytes 1310720 | tf_op jit(solution)/shard_map/all_gather | solution.py:47
  95.3 144.7 %all-gather.13.cloned.1.call-start = ((), (), s32[]{:S(2)}) async-start(), calls=%async_computation.11 | async-start | bytes 1310720 | tf_op jit(solution)/shard_map/all_gather | solution.py:47
  225.0 103.0 %all-gather.15.cloned.1.call-start = ((), (), s32[]{:S(2)}) async-start(), calls=%async_computation.12 | async-start | bytes 1310720 | tf_op jit(solution)/shard_map/all_gather | solution.py:47
  298.7 31.5 %copy-start = (f32[256,256]{1,0:T(8,128)}, f32[256,256]{1,0:T(8,128)S(1)}, u32[]{:S(2)}) copy-start(f32[256,256]{1,0:T(8,128)S(1)} %get-tuple-element.23) | copy-start | bytes 786436
Sparse Core Ops, SparseCore 0:
  48.7 15.5 all-gather.8
  95.4 14.7 all-gather.10
  225.1 14.8 all-gather.12
  313.1 14.8 all-gather.14
